TPU v7x, 32 devices: a whole 2x2x4 slice. The times are simulated.
32 devices in a mesh: band: 2 (over x), col: 16 (over z, y, core).
Axes of the slice: x: 2, y: 2, z: 4, core: 2. Of those that a mesh axis runs over, the one named last changes fastest.
Arguments:
- fields: bfloat16 [4, 80, 16, 2048], P(None, None, 'band', 'col'), may hold values from -6 to 6
- inverse: bfloat16 [4, 80, 80], replicated, may hold values from -1 to 2
- block_costs: int32 [16, 16], P('col', 'band'), may hold values from 1 to 8, as said below
- row_length: int32 [16], P('band'), may hold values from 1025 to 2048
Outputs:
- spectra: float32 [320, 16, 2, 512], P('col', None, None, 'band')
Inputs may be any that keep to these rules, and one draw needn't show every extreme that they name: `block_costs`: at least one block takes 8 substeps and at least one takes 1.
All inputs are finite; a program needn't handle non-finite values.
Results may differ from a plain program's by a relative error of at most 0.0042.
Values may be sent and summed in bfloat16 or wider, within the bound.
A program may use at most 64 MiB of HBM per device.

v0:
```python
import functools
import math

import jax
import jax.numpy as jnp
import numpy as np
from jax import lax
from jax.experimental import pallas as pl
from jax.experimental.pallas import tpu as pltpu
from jax.sharding import PartitionSpec as P

sweep_total = 8
MESH = pl.DeviceIdType.MESH


def flip(position, step, total):
    result, bit = 0, 1
    while bit < total:
        result = result + bit * (((position // bit) + (step // bit)) % 2)
        bit *= 2
    return result


def spectral_kernel(
    col_total, band_total, scale,
    cost_ref, length_ref, fields_ref, inverse_ref, base_ref, phase_ref, out_ref,
    fields_buf, turn_in, turn_out, state_ref, blocks, landed, total, outgoing, incoming, base_buf,
    field_sem, base_sem, send_sem, recv_sem, band_send, band_recv,
):
    me, band = lax.axis_index("col"), lax.axis_index("band")
    field_total, level_total, row_total, width = fields_buf.shape
    own_levels = landed.shape[1]
    piece_width = total.shape[2]
    group = col_total // field_total
    place, inside = me // group, me % group
    toward = 1 - 2 * (place // (field_total // 2))
    head = (3 * own_levels + 4) // 5
    chunks = ((0, head), (head, own_levels - head))

    def field_of(i):
        return (place + field_total + toward * (1 + i)) % field_total

    def field_copy(i):
        f = field_of(i)
        return pltpu.make_async_copy(fields_ref.at[f], fields_buf.at[i], field_sem.at[i])

    for i in range(field_total):
        field_copy(i).start()
    base_copy = pltpu.make_async_copy(base_ref, base_buf, base_sem)
    base_copy.start()
    barrier = pltpu.get_barrier_semaphore()

    def greet(t, carry):
        pl.semaphore_signal(
            barrier, inc=1, device_id={"col": (me + t) % col_total}, device_id_type=MESH
        )
        return carry

    lax.fori_loop(1, col_total, greet, 0)
    for j in range(1, band_total):
        pl.semaphore_signal(
            barrier, inc=1, device_id={"band": (band + j) % band_total}, device_id_type=MESH
        )

    costs = jnp.concatenate(
        [jnp.full((1, width), cost_ref[0, r], jnp.int32) for r in range(row_total)], axis=1
    )
    longitude = me * width + lax.broadcasted_iota(jnp.int32, (1, width), 1)
    keep = jnp.concatenate(
        [(longitude < length_ref[r]).astype(jnp.int32) for r in range(row_total)], axis=0
    )[None] > 0

    def relax(pair):
        for k in range(2):
            field_copy(2 * pair + k).wait()
            turn_in[k] = (
                fields_buf[2 * pair + k].astype(jnp.float32).reshape(level_total * row_total, width)
            )
        for k in range(2):
            for r in range(row_total):
                piece = turn_in[k, pl.ds(r, level_total, stride=row_total), :]
                state_ref[k, :, r * width : (r + 1) * width] = piece.astype(jnp.bfloat16)

        def sweep(s, carry):
            active = costs > s
            for k in range(2):
                before = state_ref[k]
                applied = jnp.dot(
                    inverse_ref[field_of(2 * pair + k)], before, preferred_element_type=jnp.float32
                )
                state_ref[k] = jnp.where(
                    active, applied, before.astype(jnp.float32)
                ).astype(jnp.bfloat16)
            return carry

        lax.fori_loop(0, sweep_total, sweep, 0, unroll=True)
        for k in range(2):
            for r in range(row_total):
                turn_out[k, pl.ds(r, level_total, stride=row_total), :] = state_ref[
                    k, :, r * width : (r + 1) * width
                ].astype(jnp.float32)
        for k in range(2):
            f = field_of(2 * pair + k)
            for q in range(group):
                rows = slice(q * own_levels * row_total, (q + 1) * own_levels * row_total)
                shape = (own_levels, row_total, width)
                initial = turn_in[k, rows, :].reshape(shape)
                tendency = (turn_out[k, rows, :].reshape(shape) - initial).astype(jnp.bfloat16)
                updated = initial + tendency.astype(jnp.float32)
                blocks[f * group + q] = jnp.where(keep, updated, 0.0).astype(jnp.bfloat16)

    def block_copy(chunk, peer, source):
        start, size = chunks[chunk]
        return pltpu.make_async_remote_copy(
            src_ref=blocks.at[peer, pl.ds(start, size)],
            dst_ref=landed.at[source, pl.ds(start, size)],
            send_sem=send_sem.at[chunk, peer],
            recv_sem=recv_sem.at[chunk, source],
            device_id={"col": peer},
            device_id_type=MESH,
        )

    def send_field(chunk, i, first):
        for j in range(first, group):
            peer = field_of(i) * group + (inside + j) % group
            block_copy(chunk, peer, me).start()

    def send_pair(chunk, pair, last):
        for i in range(2):
            send_field(chunk, 2 * pair + i, 1 if last and i == 1 else 0)

    def relax_and_send(pair, carry):
        relax(pair)
        send_pair(0, pair, False)
        return carry

    relax(0)
    pl.semaphore_wait(barrier, col_total - 1 + band_total - 1)
    send_pair(0, 0, False)
    lax.fori_loop(1, field_total // 2 - 1, relax_and_send, 0)
    relax(field_total // 2 - 1)
    send_pair(0, field_total // 2 - 1, True)

    def second_chunk(i, carry):
        send_field(1, i, 0)
        return carry

    lax.fori_loop(0, field_total - 1, second_chunk, 0)
    send_field(1, field_total - 1, 1)
    base_copy.wait()

    def rows_of(ref, source, chunk):
        start, size = chunks[chunk]
        values = ref[source, start : start + size].astype(jnp.float32)
        return values.reshape(size * row_total, width).astype(jnp.bfloat16)

    def accumulate(chunk, first_rows, second_rows, sources, fresh):
        start, size = chunks[chunk]
        held = slice(start * row_total, (start + size) * row_total)
        rows = jnp.concatenate([first_rows, second_rows], axis=1)
        for j in range(band_total):
            lanes = slice(j * piece_width, (j + 1) * piece_width)
            table = jnp.concatenate(
                [
                    (
                        base_buf[0, :, lanes] * phase_ref[source, 0:1, lanes]
                        + base_buf[1, :, lanes] * phase_ref[source, 1:2, lanes]
                    ).astype(jnp.bfloat16)
                    for source in sources
                ],
                axis=0,
            )
            value = jnp.dot(rows, table, preferred_element_type=jnp.float32)
            total[j, held] = value if fresh else total[j, held] + value

    def band_copy(chunk, j, to_peer):
        start, size = chunks[chunk]
        held = pl.ds(start * row_total, size * row_total)
        peer = (band + j) % band_total
        origin = band if to_peer else peer
        return pltpu.make_async_remote_copy(
            src_ref=outgoing.at[chunk, peer, held],
            dst_ref=incoming.at[chunk, origin, held],
            send_sem=band_send.at[chunk, peer],
            recv_sem=band_recv.at[chunk, origin],
            device_id={"band": peer},
            device_id_type=MESH,
        )

    mate = me + 1 - 2 * (me % 2)
    for chunk, (start, size) in enumerate(chunks):
        held = slice(start * row_total, (start + size) * row_total)
        block_copy(chunk, mate, mate).wait_recv()
        accumulate(
            chunk, rows_of(blocks, me, chunk), rows_of(landed, mate, chunk), (me, mate), True
        )

        def receive(t, carry):
            first = 2 * flip(me // 2, t, col_total // 2)
            block_copy(chunk, first, first).wait_recv()
            block_copy(chunk, first + 1, first + 1).wait_recv()
            accumulate(
                chunk, rows_of(landed, first, chunk), rows_of(landed, first + 1, chunk),
                (first, first + 1), False,
            )
            return carry

        lax.fori_loop(1, col_total // 2, receive, 0)
        for j in range(1, band_total):
            peer = (band + j) % band_total
            outgoing[chunk, peer, held] = (total[peer, held] * scale).astype(jnp.bfloat16)
        for j in range(1, band_total):
            band_copy(chunk, j, True).start()

    def put(origin, start, size, values):
        pieces = piece_width // 128
        for level in range(size):
            rows = values[level * row_total : (level + 1) * row_total]
            for k in range(pieces):
                out_ref[start + level, origin, pl.ds(k, row_total, stride=pieces), :] = rows[
                    :, k * 128 : (k + 1) * 128
                ]

    for start, size in chunks:
        held = slice(start * row_total, (start + size) * row_total)
        put(band, start, size, total[band, held] * scale)
    for chunk, (start, size) in enumerate(chunks):
        held = slice(start * row_total, (start + size) * row_total)
        for j in range(1, band_total):
            peer = (band + j) % band_total
            band_copy(chunk, j, False).wait_recv()
            put(peer, start, size, incoming[chunk, peer, held].astype(jnp.float32))

    def drain(t, carry):
        peer = (me + t) % col_total
        for chunk in range(len(chunks)):
            block_copy(chunk, peer, me).wait_send()
        return carry

    lax.fori_loop(1, col_total, drain, 0)
    for chunk in range(len(chunks)):
        for j in range(1, band_total):
            band_copy(chunk, j, True).wait_send()


def deliver_kernel(size, in_ref, out_ref, held, in_sem, out_sem):
    pieces = held.shape[0] // size
    parts = [pl.ds(p * size, size) for p in range(pieces)]
    reads = [
        pltpu.make_async_copy(in_ref.at[part], held.at[part], in_sem.at[p])
        for p, part in enumerate(parts)
    ]
    writes = [
        pltpu.make_async_copy(held.at[part], out_ref.at[part], out_sem.at[p])
        for p, part in enumerate(parts)
    ]
    for read in reads:
        read.start()
    for read, write in zip(reads, writes):
        read.wait()
        write.start()
    for write in writes:
        write.wait()


def tables(width, col_total, band_total):
    length = width * col_total
    waves = np.arange(length // 4, dtype=np.int64).reshape(-1, 1, 128)
    shape = (waves.shape[0], 2, 128)
    wave_of = np.broadcast_to(waves, shape).reshape(-1)
    imaginary = np.broadcast_to(np.arange(2).reshape(1, 2, 1), shape).reshape(-1)
    angle = 2.0 * np.pi * ((np.arange(width)[:, None] * wave_of[None, :]) % length) / length
    cosine, sine = np.cos(angle), np.sin(angle)
    plain = np.where(imaginary[None, :] == 1, -sine, cosine)
    crossed = np.where(imaginary[None, :] == 1, -cosine, -sine)
    base = np.stack([plain, crossed])
    turn = 2.0 * np.pi * ((np.arange(col_total)[:, None] * wave_of[None, :]) % col_total) / col_total
    phase = np.stack([np.cos(turn), np.sin(turn)], axis=1)
    return base.astype(np.float32), phase.astype(np.float32)


def shards(fields, inverse, block_costs, row_length):
    field_total, level_total, row_total, width = fields.shape
    col_total, band_total = lax.axis_size("col"), lax.axis_size("band")
    own_levels = field_total * level_total // col_total
    vmem = pl.BlockSpec(memory_space=pltpu.VMEM)
    smem = pl.BlockSpec(memory_space=pltpu.SMEM)
    hbm = pl.BlockSpec(memory_space=pl.ANY)
    base, phase = tables(width, col_total, band_total)
    own_rows, piece_width = own_levels * row_total, base.shape[2] // band_total
    waves = piece_width // 2
    spectra = pl.pallas_call(
        functools.partial(
            spectral_kernel, col_total, band_total, 1.0 / math.sqrt(width * col_total)
        ),
        name="spectral",
        out_shape=jax.ShapeDtypeStruct((own_levels, band_total, row_total * piece_width // 128, 128), jnp.float32),
        in_specs=[smem, smem, hbm, vmem, hbm, vmem],
        out_specs=vmem,
        scratch_shapes=[
            pltpu.VMEM(fields.shape, jnp.bfloat16),
            pltpu.VMEM((2, level_total * row_total, width), jnp.float32),
            pltpu.VMEM((2, level_total * row_total, width), jnp.float32),
            pltpu.VMEM((2, level_total, row_total * width), jnp.bfloat16),
            pltpu.VMEM((col_total, own_levels, row_total, width), jnp.bfloat16),
            pltpu.VMEM((col_total, own_levels, row_total, width), jnp.bfloat16),
            pltpu.VMEM((band_total, own_rows, piece_width), jnp.float32),
            pltpu.VMEM((2, band_total, own_rows, piece_width), jnp.bfloat16),
            pltpu.VMEM((2, band_total, own_rows, piece_width), jnp.bfloat16),
            pltpu.VMEM(base.shape, jnp.float32),
            pltpu.SemaphoreType.DMA((field_total,)),
            pltpu.SemaphoreType.DMA,
            pltpu.SemaphoreType.DMA((2, col_total)),
            pltpu.SemaphoreType.DMA((2, col_total)),
            pltpu.SemaphoreType.DMA((2, band_total)),
            pltpu.SemaphoreType.DMA((2, band_total)),
        ],
        compiler_params=pltpu.CompilerParams(collective_id=0, has_side_effects=True),
    )(block_costs, row_length, fields, inverse, jnp.asarray(base), jnp.asarray(phase))
    pieces = next(p for p in (5, 4, 2, 1) if own_levels % p == 0)
    spectra = pl.pallas_call(
        functools.partial(deliver_kernel, own_levels // pieces),
        name="deliver",
        out_shape=jax.ShapeDtypeStruct(spectra.shape, spectra.dtype),
        in_specs=[hbm],
        out_specs=hbm,
        scratch_shapes=[
            pltpu.VMEM(spectra.shape, spectra.dtype),
            pltpu.SemaphoreType.DMA((pieces,)),
            pltpu.SemaphoreType.DMA((pieces,)),
        ],
    )(spectra)
    split = spectra.reshape(own_levels, band_total * row_total, waves // 128, 2, 128)
    return split.transpose(0, 1, 3, 2, 4).reshape(own_levels, band_total * row_total, 2, waves)


def solution(mesh):
    return jax.shard_map(
        shards,
        mesh=mesh,
        in_specs=(P(None, None, "band", "col"), P(), P("col", "band"), P("band")),
        out_specs=P("col", None, None, "band"),
        check_vma=False,
    )
```

profile of v0, /device:TPU:0, one launch (start us, length us, event | category | flops | bytes accessed | tf_op | source)
XLA Modules:
  0.0 32.1 jit_solution(7747051889259195114)
XLA Ops:
  0.0 30.2 %spectral.1.in_ref = f32[20,2,32,128]{3,2,1,0:T(8,128)} custom-call(s32[1,8]{1,0:T(1,128)} %cost_ref.1, s32[8]{0:T(128)} %length_ref.1, bf16[4,80,8,128]{3,2,1,0:T(8,128)(2,1)} %fields_ref.1, bf16[4,80,80]{2,1,0:T(8,128)(2,1)} %inverse_ref.1, f32[2,128,1024]{2,1,0:T(8,128)} %constant.4.clone.base_ref, f32[16,2,1024]{2,1,0:T(2,128)} %constant.5.clone.phase_ref), custom_call_target="tpu_custom_call" | custom-call | tf_op jit(solution)/shard_map/spectral/pallas_call | solution.py:292
  30.2 1.9 %deliver.1 = f32[20,2,32,128]{3,2,1,0:T(8,128)} custom-call(f32[20,2,32,128]{3,2,1,0:T(8,128)} %spectral.1.in_ref), custom_call_target="tpu_custom_call" | custom-call | tf_op jit(solution)/shard_map/deliver/pallas_call | solution.py:321
where the time goes:
time: 32.3 us; the launch traced here: 32.1 us
  Pallas kernels  32.1 us (99%)
    pallas_call x1, Pallas kernels, shards(): pl.pallas_call(functools.partial(spectral_kernel, col_total, band_total,...  30.2 us
    pallas_call x1, Pallas kernels, shards(): pl.pallas_call(functools.partial(deliver_kernel, own_levels // pieces), n...  1.91 us

commit v1 on v0

v1 whole, which is shorter than its diff:
```python
import functools
import math

import jax
import jax.numpy as jnp
import numpy as np
from jax import lax
from jax.experimental import pallas as pl
from jax.experimental.pallas import tpu as pltpu
from jax.sharding import PartitionSpec as P

sweep_total = 8
field_span = 1
table_limit = 4 * 1024 * 1024
spectral_vmem = 40 * 1024 * 1024
deliver_vmem = 8 * 1024 * 1024
MESH = pl.DeviceIdType.MESH


def spectral_kernel(
    col_total, band_total, scale, chunks,
    cost_ref, length_ref, fields_ref, inverse_ref, base_ref, phase_ref, out_ref,
    cost_buf, length_buf, inverse_buf, phase_buf,
    fields_buf, turn_in, turn_out, state_ref, blocks, landed, total, outgoing, incoming, base_buf, table_buf,
    field_sem, small_sem, base_sem, send_sem, recv_sem, band_send, band_recv,
):
    me, band = lax.axis_index("col"), lax.axis_index("band")
    field_total, level_total, row_total, width = fields_buf.shape
    own_levels = landed.shape[1]
    piece_width = total.shape[2]
    span = turn_in.shape[0]
    stages = field_total // span
    group = col_total // field_total
    place, inside = me // group, me % group
    toward = 1 - 2 * (place // (field_total // 2))
    middle = ((place + 1) // 2) % 2
    keep_table = table_buf.shape[0] == col_total * width

    barrier = pltpu.get_barrier_semaphore()

    def greet(t, carry):
        pl.semaphore_signal(
            barrier, inc=1, device_id={"col": (me + t) % col_total}, device_id_type=MESH
        )
        return carry

    lax.fori_loop(1, col_total, greet, 0)
    for j in range(1, band_total):
        pl.semaphore_signal(
            barrier, inc=1, device_id={"band": (band + j) % band_total}, device_id_type=MESH
        )

    def field_of(i):
        late = i // (field_total // 2)
        offset = (1 - late) * (field_total // 2 + i) + late * (field_total - 1 - i)
        return (place + field_total + toward * offset) % field_total

    def field_copy(i):
        return pltpu.make_async_copy(fields_ref.at[field_of(i)], fields_buf.at[i], field_sem.at[i])

    small = [
        pltpu.make_async_copy(source, target, small_sem.at[n])
        for n, (source, target) in enumerate(
            (
                (cost_ref, cost_buf), (length_ref, length_buf),
                (inverse_ref, inverse_buf), (phase_ref, phase_buf),
            )
        )
    ]
    field_copy(0).start()
    for copy in small[:3]:
        copy.start()
    for i in range(1, field_total):
        field_copy(i).start()
    base_copy = pltpu.make_async_copy(base_ref, base_buf, base_sem)
    small[3].start()
    base_copy.start()

    small[0].wait()
    small[1].wait()
    costs = jnp.concatenate(
        [jnp.full((1, width), cost_buf[0, r], jnp.int32) for r in range(row_total)], axis=1
    )
    longitude = me * width + lax.broadcasted_iota(jnp.int32, (1, width), 1)
    keep = jnp.concatenate(
        [(longitude < length_buf[r]).astype(jnp.int32) for r in range(row_total)], axis=0
    )[None] > 0
    small[2].wait()

    def relax(stage):
        for k in range(span):
            field_copy(span * stage + k).wait()
            turn_in[k] = (
                fields_buf[span * stage + k].astype(jnp.float32).reshape(level_total * row_total, width)
            )
        for k in range(span):
            for r in range(row_total):
                piece = turn_in[k, pl.ds(r, level_total, stride=row_total), :]
                state_ref[k, :, r * width : (r + 1) * width] = piece.astype(jnp.bfloat16)

        def sweep(s, carry):
            active = costs > s
            for k in range(span):
                before = state_ref[k]
                applied = jnp.dot(
                    inverse_buf[field_of(span * stage + k)], before, preferred_element_type=jnp.float32
                )
                state_ref[k] = jnp.where(
                    active, applied, before.astype(jnp.float32)
                ).astype(jnp.bfloat16)
            return carry

        lax.fori_loop(0, sweep_total, sweep, 0, unroll=True)
        for k in range(span):
            for r in range(row_total):
                turn_out[k, pl.ds(r, level_total, stride=row_total), :] = state_ref[
                    k, :, r * width : (r + 1) * width
                ].astype(jnp.float32)
        for k in range(span):
            f = field_of(span * stage + k)
            for q in range(group):
                rows = slice(q * own_levels * row_total, (q + 1) * own_levels * row_total)
                shape = (own_levels, row_total, width)
                initial = turn_in[k, rows, :].reshape(shape)
                tendency = (turn_out[k, rows, :].reshape(shape) - initial).astype(jnp.bfloat16)
                updated = initial + tendency.astype(jnp.float32)
                blocks[f * group + q] = jnp.where(keep, updated, 0.0).astype(jnp.bfloat16)

    def block_copy(chunk, peer, source):
        start, size = chunks[chunk]
        return pltpu.make_async_remote_copy(
            src_ref=blocks.at[peer, pl.ds(start, size)],
            dst_ref=landed.at[source, pl.ds(start, size)],
            send_sem=send_sem.at[chunk, peer],
            recv_sem=recv_sem.at[chunk, source],
            device_id={"col": peer},
            device_id_type=MESH,
        )

    def send_field(chunk, i, first):
        for j in range(first, group):
            peer = field_of(i) * group + (inside + j) % group
            block_copy(chunk, peer, me).start()

    def send_stage(stage, last):
        for k in range(span):
            send_field(0, span * stage + k, 1 if last and k == span - 1 else 0)

    def relax_and_send(stage, carry):
        relax(stage)
        send_stage(stage, False)
        return carry

    relax(0)
    pl.semaphore_wait(barrier, col_total - 1 + band_total - 1)
    send_stage(0, False)
    lax.fori_loop(1, stages - 1, relax_and_send, 0)
    relax(stages - 1)
    send_stage(stages - 1, True)

    for chunk in range(1, len(chunks)):
        def send_later(i, carry, chunk=chunk):
            send_field(chunk, i, 0)
            return carry

        lax.fori_loop(0, field_total - 1, send_later, 0)
        send_field(chunk, field_total - 1, 1)
    landed[me] = blocks[me]
    small[3].wait()
    base_copy.wait()

    def rows_of(source, chunk):
        start, size = chunks[chunk]
        values = landed[source, start : start + size].astype(jnp.float32)
        return values.reshape(size * row_total, width).astype(jnp.bfloat16)

    def accumulate(chunk, first, fresh):
        start, size = chunks[chunk]
        held = slice(start * row_total, (start + size) * row_total)
        rows = jnp.concatenate([rows_of(first, chunk), rows_of(first + 1, chunk)], axis=1)
        place_held = pl.ds(pl.multiple_of(first * width, width), 2 * width)
        for j in range(band_total):
            lanes = slice(j * piece_width, (j + 1) * piece_width)
            if keep_table and chunk > 0:
                table = table_buf[place_held, lanes]
            else:
                table = jnp.concatenate(
                    [
                        (
                            base_buf[0, :, lanes] * phase_buf[first + k, 0:1, lanes]
                            + base_buf[1, :, lanes] * phase_buf[first + k, 1:2, lanes]
                        ).astype(jnp.bfloat16)
                        for k in range(2)
                    ],
                    axis=0,
                )
                if keep_table:
                    table_buf[place_held, lanes] = table
            value = jnp.dot(rows, table, preferred_element_type=jnp.float32)
            total[j, held] = value if fresh else total[j, held] + value

    def band_copy(chunk, j, to_peer):
        start, size = chunks[chunk]
        held = pl.ds(start * row_total, size * row_total)
        peer = (band + j) % band_total
        origin = band if to_peer else peer
        return pltpu.make_async_remote_copy(
            src_ref=outgoing.at[peer, held],
            dst_ref=incoming.at[origin, held],
            send_sem=band_send.at[chunk, peer],
            recv_sem=band_recv.at[chunk, origin],
            device_id={"band": peer},
            device_id_type=MESH,
        )

    pairs = group // 2

    def first_of(t):
        g = t // pairs
        moved = ((g + field_total - 1) // field_total) * (g % (field_total - 1) + 1)
        offset = (1 - middle) * g + middle * moved
        source_place = (place + field_total + toward * offset) % field_total
        return source_place * group + 2 * ((inside // 2 + t % pairs) % pairs)

    mate = me + 1 - 2 * (me % 2)
    for chunk, (start, size) in enumerate(chunks):
        held = slice(start * row_total, (start + size) * row_total)
        block_copy(chunk, mate, mate).wait_recv()
        accumulate(chunk, first_of(0), True)

        def receive(t, carry, chunk=chunk):
            first = first_of(t)
            block_copy(chunk, first, first).wait_recv()
            block_copy(chunk, first + 1, first + 1).wait_recv()
            accumulate(chunk, first, False)
            return carry

        lax.fori_loop(1, col_total // 2, receive, 0)
        for j in range(1, band_total):
            peer = (band + j) % band_total
            outgoing[peer, held] = (total[peer, held] * scale).astype(jnp.bfloat16)
        for j in range(1, band_total):
            band_copy(chunk, j, True).start()

    def put(origin, start, size, values):
        pieces = piece_width // 128
        for level in range(size):
            rows = values[level * row_total : (level + 1) * row_total]
            for k in range(pieces):
                out_ref[start + level, origin, pl.ds(k, row_total, stride=pieces), :] = rows[
                    :, k * 128 : (k + 1) * 128
                ]

    for start, size in chunks:
        held = slice(start * row_total, (start + size) * row_total)
        put(band, start, size, total[band, held] * scale)

    def drain(t, carry):
        peer = (me + t) % col_total
        for chunk in range(len(chunks)):
            block_copy(chunk, peer, me).wait_send()
        return carry

    lax.fori_loop(1, col_total, drain, 0)
    for chunk, (start, size) in enumerate(chunks):
        held = slice(start * row_total, (start + size) * row_total)
        for j in range(1, band_total):
            peer = (band + j) % band_total
            band_copy(chunk, j, False).wait_recv()
            put(peer, start, size, incoming[peer, held].astype(jnp.float32))
    for chunk in range(len(chunks)):
        for j in range(1, band_total):
            band_copy(chunk, j, True).wait_send()


def deliver_kernel(size, held, out_ref, out_sem):
    parts = [pl.ds(p * size, size) for p in range(held.shape[0] // size)]
    writes = [
        pltpu.make_async_copy(held.at[part], out_ref.at[part], out_sem.at[p])
        for p, part in enumerate(parts)
    ]
    for write in writes:
        write.start()
    for write in writes:
        write.wait()


def level_chunks(own_levels):
    last = max(1, own_levels // 5)
    head = (own_levels - last + 1) // 2
    sizes = [n for n in (head, own_levels - last - head, last) if n > 0]
    return tuple((sum(sizes[:i]), n) for i, n in enumerate(sizes))


def tables(width, col_total, band_total):
    length = width * col_total
    waves = np.arange(length // 4, dtype=np.int64).reshape(-1, 1, 128)
    shape = (waves.shape[0], 2, 128)
    wave_of = np.broadcast_to(waves, shape).reshape(-1)
    imaginary = np.broadcast_to(np.arange(2).reshape(1, 2, 1), shape).reshape(-1)
    angle = 2.0 * np.pi * ((np.arange(width)[:, None] * wave_of[None, :]) % length) / length
    cosine, sine = np.cos(angle), np.sin(angle)
    plain = np.where(imaginary[None, :] == 1, -sine, cosine)
    crossed = np.where(imaginary[None, :] == 1, -cosine, -sine)
    base = np.stack([plain, crossed])
    turn = 2.0 * np.pi * ((np.arange(col_total)[:, None] * wave_of[None, :]) % col_total) / col_total
    phase = np.stack([np.cos(turn), np.sin(turn)], axis=1)
    return base.astype(np.float32), phase.astype(np.float32)


def shards(fields, inverse, block_costs, row_length):
    field_total, level_total, row_total, width = fields.shape
    col_total, band_total = lax.axis_size("col"), lax.axis_size("band")
    own_levels = field_total * level_total // col_total
    vmem = pl.BlockSpec(memory_space=pltpu.VMEM)
    hbm = pl.BlockSpec(memory_space=pl.ANY)
    base, phase = tables(width, col_total, band_total)
    own_rows, piece_width = own_levels * row_total, base.shape[2] // band_total
    waves = piece_width // 2
    chunks = level_chunks(own_levels)
    table_shape = (col_total * width, base.shape[2])
    if table_shape[0] * table_shape[1] > table_limit:
        table_shape = (16, 128)
    shape = (own_levels, band_total, row_total * piece_width // 128, 128)
    spectra = pl.pallas_call(
        functools.partial(
            spectral_kernel, col_total, band_total, 1.0 / math.sqrt(width * col_total), chunks
        ),
        name="spectral",
        out_shape=pltpu.VMEM(shape, jnp.float32),
        in_specs=[hbm] * 6,
        out_specs=vmem,
        scratch_shapes=[
            pltpu.SMEM(block_costs.shape, jnp.int32),
            pltpu.SMEM(row_length.shape, jnp.int32),
            pltpu.VMEM(inverse.shape, jnp.bfloat16),
            pltpu.VMEM(phase.shape, jnp.float32),
            pltpu.VMEM(fields.shape, jnp.bfloat16),
            pltpu.VMEM((field_span, level_total * row_total, width), jnp.float32),
            pltpu.VMEM((field_span, level_total * row_total, width), jnp.float32),
            pltpu.VMEM((field_span, level_total, row_total * width), jnp.bfloat16),
            pltpu.VMEM((col_total, own_levels, row_total, width), jnp.bfloat16),
            pltpu.VMEM((col_total, own_levels, row_total, width), jnp.bfloat16),
            pltpu.VMEM((band_total, own_rows, piece_width), jnp.float32),
            pltpu.VMEM((band_total, own_rows, piece_width), jnp.bfloat16),
            pltpu.VMEM((band_total, own_rows, piece_width), jnp.bfloat16),
            pltpu.VMEM(base.shape, jnp.float32),
            pltpu.VMEM(table_shape, jnp.bfloat16),
            pltpu.SemaphoreType.DMA((field_total,)),
            pltpu.SemaphoreType.DMA((4,)),
            pltpu.SemaphoreType.DMA,
            pltpu.SemaphoreType.DMA((len(chunks), col_total)),
            pltpu.SemaphoreType.DMA((len(chunks), col_total)),
            pltpu.SemaphoreType.DMA((len(chunks), band_total)),
            pltpu.SemaphoreType.DMA((len(chunks), band_total)),
        ],
        compiler_params=pltpu.CompilerParams(
            collective_id=0, has_side_effects=True, vmem_limit_bytes=spectral_vmem
        ),
    )(
        *(
            pltpu.with_memory_space_constraint(value, pltpu.HBM)
            for value in (block_costs, row_length, fields, inverse, jnp.asarray(base), jnp.asarray(phase))
        )
    )
    pieces = next(p for p in (5, 4, 2, 1) if own_levels % p == 0)
    spectra = pl.pallas_call(
        functools.partial(deliver_kernel, own_levels // pieces),
        name="deliver",
        out_shape=jax.ShapeDtypeStruct(spectra.shape, spectra.dtype),
        in_specs=[vmem],
        out_specs=hbm,
        scratch_shapes=[pltpu.SemaphoreType.DMA((pieces,))],
        compiler_params=pltpu.CompilerParams(vmem_limit_bytes=deliver_vmem),
    )(spectra)
    split = spectra.reshape(own_levels, band_total * row_total, waves // 128, 2, 128)
    return split.transpose(0, 1, 3, 2, 4).reshape(own_levels, band_total * row_total, 2, waves)


def solution(mesh):
    return jax.shard_map(
        shards,
        mesh=mesh,
        in_specs=(P(None, None, "band", "col"), P(), P("col", "band"), P("band")),
        out_specs=P("col", None, None, "band"),
        check_vma=False,
    )
```

time: 32.3 us -> 28 us (0.87)
  Pallas kernels: 32.1 us -> 27.8 us
    pallas_call x1, Pallas kernels: 30.2 us -> 26.9 us  [shards(): pl.pallas_call(functools.partial(spectral_kernel, col_total, band_total,...]
    pallas_call x1, Pallas kernels: 1.91 us -> 0.87 us  [shards(): pl.pallas_call(functools.partial(deliver_kernel, own_levels // pieces), n...]
where the time goes in v1:
time: 28 us; the launch traced here: 27.8 us
  Pallas kernels  27.8 us (99%)
    pallas_call x1, Pallas kernels, shards(): pl.pallas_call(functools.partial(spectral_kernel, col_total, band_total,...  26.9 us
    pallas_call x1, Pallas kernels, shards(): pl.pallas_call(functools.partial(deliver_kernel, own_levels // pieces), n...  0.87 us

profile of v1, /device:TPU:0, one launch (start us, length us, event | category | flops | bytes accessed | tf_op | source)
XLA Modules:
  0.0 27.8 jit_solution(8258489760807474463)
XLA Ops:
  0.0 26.9 %spectral.1.held = f32[20,2,32,128]{3,2,1,0:T(8,128)S(1)} custom-call(s32[1,8]{1,0:T(1,128)} %cost_ref.1, s32[8]{0:T(128)} %length_ref.1, bf16[4,80,8,128]{3,2,1,0:T(8,128)(2,1)} %fields_ref.1, bf16[4,80,80]{2,1,0:T(8,128)(2,1)} %inverse_ref.1, f32[2,128,1024]{2,1,0:T(8,128)} %constant.4.clone.base_ref, f32[16,2,1024]{2,1,0:T(2,128)} %constant.5.clone.phase_ref), custom_call_target="tpu_custom_call" | custom-call | tf_op jit(solution)/shard_map/spectral/pallas_call | solution.py:325
  26.9 0.9 %deliver.1 = f32[20,2,32,128]{3,2,1,0:T(8,128)} custom-call(f32[20,2,32,128]{3,2,1,0:T(8,128)S(1)} %spectral.1.held), custom_call_target="tpu_custom_call" | custom-call | tf_op jit(solution)/shard_map/deliver/pallas_call | solution.py:367

commit v2 on v1

--- a/solution.py
+++ b/solution.py
@@ -10,7 +10,7 @@
 from jax.sharding import PartitionSpec as P
 
 sweep_total = 8
-field_span = 1
+field_span = 2
 table_limit = 4 * 1024 * 1024
 spectral_vmem = 40 * 1024 * 1024
 deliver_vmem = 8 * 1024 * 1024
@@ -34,6 +34,7 @@
     place, inside = me // group, me % group
     toward = 1 - 2 * (place // (field_total // 2))
     middle = ((place + 1) // 2) % 2
+    batch = min(group, 4)
     keep_table = table_buf.shape[0] == col_total * width
 
     barrier = pltpu.get_barrier_semaphore()
@@ -131,20 +132,21 @@
         return pltpu.make_async_remote_copy(
             src_ref=blocks.at[peer, pl.ds(start, size)],
             dst_ref=landed.at[source, pl.ds(start, size)],
-            send_sem=send_sem.at[chunk, peer],
-            recv_sem=recv_sem.at[chunk, source],
+            send_sem=send_sem,
+            recv_sem=recv_sem.at[chunk, source // batch],
             device_id={"col": peer},
             device_id_type=MESH,
         )
 
-    def send_field(chunk, i, first):
-        for j in range(first, group):
-            peer = field_of(i) * group + (inside + j) % group
-            block_copy(chunk, peer, me).start()
+    def send_field(chunk_set, i, first):
+        for chunk in chunk_set:
+            for j in range(first, group):
+                peer = field_of(i) * group + (inside + j) % group
+                block_copy(chunk, peer, me).start()
 
     def send_stage(stage, last):
         for k in range(span):
-            send_field(0, span * stage + k, 1 if last and k == span - 1 else 0)
+            send_field((0,), span * stage + k, 1 if last and k == span - 1 else 0)
 
     def relax_and_send(stage, carry):
         relax(stage)
@@ -157,14 +159,14 @@
     lax.fori_loop(1, stages - 1, relax_and_send, 0)
     relax(stages - 1)
     send_stage(stages - 1, True)
-
-    for chunk in range(1, len(chunks)):
-        def send_later(i, carry, chunk=chunk):
-            send_field(chunk, i, 0)
-            return carry
-
-        lax.fori_loop(0, field_total - 1, send_later, 0)
-        send_field(chunk, field_total - 1, 1)
+    later = range(1, len(chunks))
+
+    def send_later(i, carry):
+        send_field(later, i, 0)
+        return carry
+
+    lax.fori_loop(0, field_total - 1, send_later, 0)
+    send_field(later, field_total - 1, 1)
     landed[me] = blocks[me]
     small[3].wait()
     base_copy.wait()
@@ -177,12 +179,12 @@
     def accumulate(chunk, first, fresh):
         start, size = chunks[chunk]
         held = slice(start * row_total, (start + size) * row_total)
-        rows = jnp.concatenate([rows_of(first, chunk), rows_of(first + 1, chunk)], axis=1)
-        place_held = pl.ds(pl.multiple_of(first * width, width), 2 * width)
+        rows = jnp.concatenate([rows_of(first + k, chunk) for k in range(batch)], axis=1)
         for j in range(band_total):
             lanes = slice(j * piece_width, (j + 1) * piece_width)
+            kept = pl.ds(pl.multiple_of(first * width, batch * width), batch * width)
             if keep_table and chunk > 0:
-                table = table_buf[place_held, lanes]
+                table = table_buf[kept, lanes]
             else:
                 table = jnp.concatenate(
                     [
@@ -190,12 +192,12 @@
                             base_buf[0, :, lanes] * phase_buf[first + k, 0:1, lanes]
                             + base_buf[1, :, lanes] * phase_buf[first + k, 1:2, lanes]
                         ).astype(jnp.bfloat16)
-                        for k in range(2)
+                        for k in range(batch)
                     ],
                     axis=0,
                 )
                 if keep_table:
-                    table_buf[place_held, lanes] = table
+                    table_buf[kept, lanes] = table
             value = jnp.dot(rows, table, preferred_element_type=jnp.float32)
             total[j, held] = value if fresh else total[j, held] + value
 
@@ -213,34 +215,55 @@
             device_id_type=MESH,
         )
 
-    pairs = group // 2
-
-    def first_of(t):
-        g = t // pairs
+    batches = group // batch
+
+    def first_of(g, t):
         moved = ((g + field_total - 1) // field_total) * (g % (field_total - 1) + 1)
         offset = (1 - middle) * g + middle * moved
         source_place = (place + field_total + toward * offset) % field_total
-        return source_place * group + 2 * ((inside // 2 + t % pairs) % pairs)
-
-    mate = me + 1 - 2 * (me % 2)
-    for chunk, (start, size) in enumerate(chunks):
+        return source_place * group + batch * ((inside // batch + t) % batches)
+
+    def await_blocks(chunk, source, first, count):
+        start, size = chunks[chunk]
+        blocks_in = landed.at[pl.ds(first, count), pl.ds(start, size)]
+        pltpu.make_async_copy(blocks_in, blocks_in, recv_sem.at[chunk, source // batch]).wait()
+
+    def receive(chunk, g, t):
+        first = first_of(g, t)
+        await_blocks(chunk, first, first, batch)
+        accumulate(chunk, first, False)
+
+    def receive_group(chunk, g):
+        if g == 0:
+            await_blocks(chunk, me, 0, batch - 1)
+            accumulate(chunk, first_of(0, 0), True)
+        first_step = 1 if g == 0 else 0
+        if batches - first_step == 1:
+            receive(chunk, g, first_step)
+        elif batches - first_step > 1:
+
+            def body(t, carry):
+                receive(chunk, g, t)
+                return carry
+
+            lax.fori_loop(first_step, batches, body, 0)
+
+    def hand_over(chunk):
+        start, size = chunks[chunk]
         held = slice(start * row_total, (start + size) * row_total)
-        block_copy(chunk, mate, mate).wait_recv()
-        accumulate(chunk, first_of(0), True)
-
-        def receive(t, carry, chunk=chunk):
-            first = first_of(t)
-            block_copy(chunk, first, first).wait_recv()
-            block_copy(chunk, first + 1, first + 1).wait_recv()
-            accumulate(chunk, first, False)
-            return carry
-
-        lax.fori_loop(1, col_total // 2, receive, 0)
         for j in range(1, band_total):
             peer = (band + j) % band_total
             outgoing[peer, held] = (total[peer, held] * scale).astype(jnp.bfloat16)
         for j in range(1, band_total):
             band_copy(chunk, j, True).start()
+
+    order = [(0, g) for g in range(field_total)]
+    order += [(chunk, g) for g in range(field_total // 2) for chunk in later]
+    order += [(chunk, g) for chunk in later for g in range(field_total // 2, field_total)]
+    for chunk, g in order:
+        receive_group(chunk, g)
+        if g == field_total - 1:
+            hand_over(chunk)
 
     def put(origin, start, size, values):
         pieces = piece_width // 128
@@ -255,13 +278,8 @@
         held = slice(start * row_total, (start + size) * row_total)
         put(band, start, size, total[band, held] * scale)
 
-    def drain(t, carry):
-        peer = (me + t) % col_total
-        for chunk in range(len(chunks)):
-            block_copy(chunk, peer, me).wait_send()
-        return carry
-
-    lax.fori_loop(1, col_total, drain, 0)
+    sent = blocks.at[pl.ds(0, col_total - 1)]
+    pltpu.make_async_copy(sent, sent, send_sem).wait()
     for chunk, (start, size) in enumerate(chunks):
         held = slice(start * row_total, (start + size) * row_total)
         for j in range(1, band_total):
@@ -287,9 +305,8 @@
 
 def level_chunks(own_levels):
     last = max(1, own_levels // 5)
-    head = (own_levels - last + 1) // 2
-    sizes = [n for n in (head, own_levels - last - head, last) if n > 0]
-    return tuple((sum(sizes[:i]), n) for i, n in enumerate(sizes))
+    sizes = [own_levels - 2 * last, last, last]
+    return tuple((sum(sizes[:i]), n) for i, n in enumerate(sizes) if n > 0)
 
 
 def tables(width, col_total, band_total):
@@ -349,8 +366,8 @@
             pltpu.SemaphoreType.DMA((field_total,)),
             pltpu.SemaphoreType.DMA((4,)),
             pltpu.SemaphoreType.DMA,
-            pltpu.SemaphoreType.DMA((len(chunks), col_total)),
-            pltpu.SemaphoreType.DMA((len(chunks), col_total)),
+            pltpu.SemaphoreType.DMA,
+            pltpu.SemaphoreType.DMA((len(chunks), col_total // min(col_total // field_total, 4))),
             pltpu.SemaphoreType.DMA((len(chunks), band_total)),
             pltpu.SemaphoreType.DMA((len(chunks), band_total)),
         ],

time: 28 us -> 27.1 us (0.968)
  Pallas kernels: 27.8 us -> 26.9 us
    pallas_call x1, Pallas kernels: 26.9 us -> 26.1 us  [shards(): pl.pallas_call(functools.partial(spectral_kernel, col_total, band_total,...]
where the time goes in v2:
time: 27.1 us; the launch traced here: 26.9 us
  Pallas kernels  26.9 us (99%)
    pallas_call x1, Pallas kernels, shards(): pl.pallas_call(functools.partial(spectral_kernel, col_total, band_total,...  26.1 us
    pallas_call x1, Pallas kernels, shards(): pl.pallas_call(functools.partial(deliver_kernel, own_levels // pieces), n...  0.87 us

profile of v2, /device:TPU:0, one launch (start us, length us, event | category | flops | bytes accessed | tf_op | source)
XLA Modules:
  0.0 26.9 jit_solution(6866736196399293701)
XLA Ops:
  0.0 26.1 %spectral.1.held = f32[20,2,32,128]{3,2,1,0:T(8,128)S(1)} custom-call(s32[1,8]{1,0:T(1,128)} %cost_ref.1, s32[8]{0:T(128)} %length_ref.1, bf16[4,80,8,128]{3,2,1,0:T(8,128)(2,1)} %fields_ref.1, bf16[4,80,80]{2,1,0:T(8,128)(2,1)} %inverse_ref.1, f32[2,128,1024]{2,1,0:T(8,128)} %constant.4.clone.base_ref, f32[16,2,1024]{2,1,0:T(2,128)} %constant.5.clone.phase_ref), custom_call_target="tpu_custom_call" | custom-call | tf_op jit(solution)/shard_map/spectral/pallas_call | solution.py:342
  26.1 0.9 %deliver.1 = f32[20,2,32,128]{3,2,1,0:T(8,128)} custom-call(f32[20,2,32,128]{3,2,1,0:T(8,128)S(1)} %spectral.1.held), custom_call_target="tpu_custom_call" | custom-call | tf_op jit(solution)/shard_map/deliver/pallas_call | solution.py:384

commit v3 on v2

--- a/solution.py
+++ b/solution.py
@@ -11,6 +11,8 @@
 
 sweep_total = 8
 field_span = 2
+far_after = 2
+near_after = 3
 table_limit = 4 * 1024 * 1024
 spectral_vmem = 40 * 1024 * 1024
 deliver_vmem = 8 * 1024 * 1024
@@ -161,12 +163,11 @@
     send_stage(stages - 1, True)
     later = range(1, len(chunks))
 
+
     def send_later(i, carry):
         send_field(later, i, 0)
         return carry
 
-    lax.fori_loop(0, field_total - 1, send_later, 0)
-    send_field(later, field_total - 1, 1)
     landed[me] = blocks[me]
     small[3].wait()
     base_copy.wait()
@@ -262,6 +263,11 @@
     order += [(chunk, g) for chunk in later for g in range(field_total // 2, field_total)]
     for chunk, g in order:
         receive_group(chunk, g)
+        if (chunk, g) == (0, far_after):
+            lax.fori_loop(0, field_total // 2, send_later, 0)
+        if (chunk, g) == (0, near_after):
+            lax.fori_loop(field_total // 2, field_total - 1, send_later, 0)
+            send_field(later, field_total - 1, 1)
         if g == field_total - 1:
             hand_over(chunk)
 

time: 27.1 us -> 27.3 us (level)
  Pallas kernels: 26.9 us -> 27.2 us
where the time goes in v3:
time: 27.3 us; the launch traced here: 27.2 us
  Pallas kernels  27.2 us (100%)
    pallas_call x1, Pallas kernels, shards(): pl.pallas_call(functools.partial(spectral_kernel, col_total, band_total,...  26.3 us
    pallas_call x1, Pallas kernels, shards(): pl.pallas_call(functools.partial(deliver_kernel, own_levels // pieces), n...  0.87 us

profile of v3, /device:TPU:0, one launch (start us, length us, event | category | flops | bytes accessed | tf_op | source)
XLA Modules:
  0.0 27.2 jit_solution(5046487415837618256)
XLA Ops:
  0.0 26.3 %spectral.1.held = f32[20,2,32,128]{3,2,1,0:T(8,128)S(1)} custom-call(s32[1,8]{1,0:T(1,128)} %cost_ref.1, s32[8]{0:T(128)} %length_ref.1, bf16[4,80,8,128]{3,2,1,0:T(8,128)(2,1)} %fields_ref.1, bf16[4,80,80]{2,1,0:T(8,128)(2,1)} %inverse_ref.1, f32[2,128,1024]{2,1,0:T(8,128)} %constant.4.clone.base_ref, f32[16,2,1024]{2,1,0:T(2,128)} %constant.5.clone.phase_ref), custom_call_target="tpu_custom_call" | custom-call | tf_op jit(solution)/shard_map/spectral/pallas_call | solution.py:348
  26.3 0.9 %deliver.1 = f32[20,2,32,128]{3,2,1,0:T(8,128)} custom-call(f32[20,2,32,128]{3,2,1,0:T(8,128)S(1)} %spectral.1.held), custom_call_target="tpu_custom_call" | custom-call | tf_op jit(solution)/shard_map/deliver/pallas_call | solution.py:390
